TPU v7x, 256 devices: a whole 4x4x8 slice. The times are simulated.
256 devices in a mesh: island: 4 (over z_hi, core), tensor: 64 (over y, x, z_lo).
Axes of the slice: x: 4, y: 4, z: 8 (z_hi: 2, z_lo: 4; z = z_hi * 4 + z_lo), core: 2. Of those that a mesh axis runs over, the one named last changes fastest.
Arguments:
- activations: bfloat16 [4, 1024, 5120], P('island', 'tensor'), may hold values from -30 to 30, as said below
- cotangent: bfloat16 [4, 1024, 5120], P('island', 'tensor'), may hold values from -24 to 24
- gate_weight: bfloat16 [4, 6912, 5120], P('island', 'tensor'), may hold values from -6 to 6
- up_weight: bfloat16 [4, 6912, 5120], P('island', 'tensor'), may hold values from -6 to 6
- down_weight: bfloat16 [4, 6912, 5120], P('island', 'tensor'), may hold values from -6 to 6
- gate_control: bfloat16 [4, 6912, 5120], P('island', 'tensor'), may hold values from -4 to 4
- up_control: bfloat16 [4, 6912, 5120], P('island', 'tensor'), may hold values from -4 to 4
- down_control: bfloat16 [4, 6912, 5120], P('island', 'tensor'), may hold values from -4 to 4
Outputs:
- gate_new: bfloat16 [6912, 5120], P('tensor')
- up_new: bfloat16 [6912, 5120], P('tensor')
- down_new: bfloat16 [6912, 5120], P('tensor')
- gate_control_new: bfloat16 [4, 6912, 5120], P('island', 'tensor')
- up_control_new: bfloat16 [4, 6912, 5120], P('island', 'tensor')
- down_control_new: bfloat16 [4, 6912, 5120], P('island', 'tensor')
Inputs may be any that keep to these rules, and one draw needn't show every extreme that they name: `activations`: real values; columns and tokens carry different scales.
All inputs are finite; a program needn't handle non-finite values.
Results may differ from a plain program's by a relative error of at most 0.0095.
Values may be sent and summed in bfloat16 or wider, within the bound.
No kernel may reach another device: no remote copies, remote signals or barrier semaphores. Data moves between devices by JAX's collectives and lax.ppermute only.
A program may use at most 128 MiB of HBM per device.

v0:
```python
import jax
import jax.numpy as jnp
from jax import lax
from jax.sharding import PartitionSpec as P

D = 5120
FF = 6912
EPSILON = 1e-06
STEP_SIZE = 1.0
PROX_PROB = 0.5


def contract_first(left, right):
    return lax.dot_general(
        left, right, (((0,), (0,)), ((), ())), preferred_element_type=jnp.float32
    )


def contract_last(left, right):
    return lax.dot_general(
        left, right, (((1,), (1,)), ((), ())), preferred_element_type=jnp.float32
    )


def normalize(rows):
    wide = rows.astype(jnp.float32)
    mean_square = jnp.mean(wide * wide, axis=-1, keepdims=True)
    return (wide * lax.rsqrt(mean_square + EPSILON)).astype(jnp.bfloat16)


def block_grads(normed, cot_rows, gate_w, up_w, down_w):
    d_scale = D ** (-0.5)
    f_scale = FF ** (-0.5)
    gate_proj = contract_last(normed, gate_w) * d_scale
    up_proj = contract_last(normed, up_w) * d_scale
    sigmoid_gate = jax.nn.sigmoid(gate_proj)
    activated = gate_proj * sigmoid_gate
    hidden = (activated * up_proj).astype(jnp.bfloat16)
    grad_down = contract_first(hidden, cot_rows) * f_scale
    grad_hidden = contract_last(cot_rows, down_w) * f_scale
    grad_gatepre = (
        grad_hidden * up_proj * sigmoid_gate * (1.0 + gate_proj * (1.0 - sigmoid_gate))
    ).astype(jnp.bfloat16)
    grad_uppre = (grad_hidden * activated).astype(jnp.bfloat16)
    grad_gate = contract_first(grad_gatepre, normed) * d_scale
    grad_up = contract_first(grad_uppre, normed) * d_scale
    return (grad_gate, grad_up, grad_down)


def prox_parts(weight, control, grad):
    control_wide = control.astype(jnp.float32)
    local = weight.astype(jnp.float32) - STEP_SIZE * (grad - control_wide)
    return (local, (local - STEP_SIZE / PROX_PROB * control_wide).astype(jnp.bfloat16))


def fresh_control(control, mean_rounded, local):
    wide = control.astype(jnp.float32) + PROX_PROB / STEP_SIZE * (
        mean_rounded.astype(jnp.float32) - local
    )
    return wide.astype(jnp.bfloat16)[None]


def per_device(
    activations,
    cotangent,
    gate_weight,
    up_weight,
    down_weight,
    gate_control,
    up_control,
    down_control,
):
    own_rows = activations[0]
    own_cot = cotangent[0]
    normed = lax.all_gather(normalize(own_rows), "tensor", axis=0, tiled=True)
    whole_cot = lax.all_gather(own_cot, "tensor", axis=0, tiled=True)
    grad_gate, grad_up, grad_down = block_grads(
        normed, whole_cot, gate_weight[0], up_weight[0], down_weight[0]
    )
    local_gate, term_gate = prox_parts(gate_weight[0], gate_control[0], grad_gate)
    local_up, term_up = prox_parts(up_weight[0], up_control[0], grad_up)
    local_down, term_down = prox_parts(down_weight[0], down_control[0], grad_down)
    count = lax.axis_size("island")
    total_gate, total_up, total_down = (
        lax.psum(term_gate, "island").astype(jnp.float32),
        lax.psum(term_up, "island").astype(jnp.float32),
        lax.psum(term_down, "island").astype(jnp.float32),
    )
    mean_gate = (total_gate / count).astype(jnp.bfloat16)
    mean_up = (total_up / count).astype(jnp.bfloat16)
    mean_down = (total_down / count).astype(jnp.bfloat16)
    new_gate_control = fresh_control(gate_control[0], mean_gate, local_gate)
    new_up_control = fresh_control(up_control[0], mean_up, local_up)
    new_down_control = fresh_control(down_control[0], mean_down, local_down)
    return (mean_gate, mean_up, mean_down, new_gate_control, new_up_control, new_down_control)


def solution(mesh):
    placed = (
        P("island", "tensor", None),
        P("island", "tensor", None),
        P("island", "tensor", None),
        P("island", "tensor", None),
        P("island", "tensor", None),
        P("island", "tensor", None),
        P("island", "tensor", None),
        P("island", "tensor", None),
    )
    return jax.shard_map(
        per_device,
        mesh=mesh,
        in_specs=placed,
        out_specs=(
            P("tensor", None),
            P("tensor", None),
            P("tensor", None),
            P("island", "tensor", None),
            P("island", "tensor", None),
            P("island", "tensor", None),
        ),
        check_vma=False,
    )
```

profile of v0, /device:TPU:1, one launch (start us, length us, event | category | flops | bytes accessed | tf_op | source)
XLA Modules:
  0.0 956.3 jit_solution(8239383202195098988)
XLA Ops:
  7.2 0.0 all-gather.4.cloned.1.call-start
  7.2 1.1 fusion.36
  8.3 1.7 fusion.37
  10.0 0.0 all-gather.4.cloned.1.call-update
  10.0 0.0 all-gather.6.cloned.1.call-start
  10.0 0.7 all-gather.6.cloned.1.call-update
  10.8 0.0 copy-start.11
  10.8 0.0 all-reduce.3.cloned.1.call-start
  10.8 343.7 %all-gather.4.cloned.1.call-done = bf16[1024,5120]{1,0:T(8,128)(2,1)} async-done(((bf16[16,5120]{1,0:T(8,128)(2,1)}), bf16[1024,5120]{1,0:T(8,128)(2,1)}) %all-gather.4.cloned.1.call-update) | async-done | bytes 10485776 | tf_op jit(solution)/shard_map/all_gather | solution.py:75
  354.5 7.9 convolution_multiply_fusion.2
  362.4 0.0 copy-start.8
  362.4 3.5 convolution_multiply_fusion.3
  366.0 367.8 %all-gather.6.cloned.1.call-done = bf16[1,1024,5120]{2,1,0:T(8,128)(2,1)} async-done(((bf16[1,16,5120]{2,1,0:T(8,128)(2,1)}), bf16[1,1024,5120]{2,1,0:T(8,128)(2,1)}) %all-gather.6.cloned.1.call-update) | async-done | bytes 10485776 | tf_op jit(solution)/shard_map/all_gather | solution.py:76
  733.8 7.6 fusion.26
  741.4 0.0 copy-start.2
  741.4 7.5 fusion.24
  749.0 0.0 copy-start.4
  749.0 4.4 fusion.18
  753.4 4.5 fusion.21
  757.8 0.0 all-reduce.3.cloned.1.call-update
  757.9 184.1 %all-reduce.3.cloned.1.call-done = (bf16[108,5120]{1,0:T(8,128)(2,1)}, bf16[108,5120]{1,0:T(8,128)(2,1)}, bf16[108,5120]{1,0:T(8,128)(2,1)}) async-done(((bf16[108,5120]{1,0:T(8,128)(2,1)}, bf16[108,5120]{1,0:T(8,128)(2,1)}, bf16[108,5120]{1,0:T(8,128)(2,1)}), (bf16[108,5120]{1,0:T(8,128)(2,1)}, bf16[108,5120]{1,0:T(8,128)(2,1)}, bf16[108,5120]{1,0:T(8,128)(2,1)})) %all-reduce.3.cloned.1.call-update) | async-done | bytes 3317776 | tf_op jit(solution)/shard_map/psum | solution.py:85
  942.0 4.0 fusion.31
  946.0 0.7 copy-done.14
  946.8 3.0 fusion.29
  (33 shorter events, 0.1 us)
Async XLA Ops:
  7.2 347.3 %all-gather.4.cloned.1.call-start = ((), (), s32[]{:S(2)}) async-start(), calls=%async_computation | async-start | bytes 10649600 | tf_op jit(solution)/shard_map/all_gather | solution.py:75
  10.0 723.7 %all-gather.6.cloned.1.call-start = ((), (), s32[]{:S(2)}) async-start(), calls=%async_computation.1 | async-start | bytes 10649600 | tf_op jit(solution)/shard_map/all_gather | solution.py:76
  10.8 351.7 %copy-start.11 = (bf16[1,108,5120]{2,1,0:T(8,128)(2,1)S(1)}, bf16[1,108,5120]{2,1,0:T(8,128)(2,1)}, u32[]{:S(2)}) copy-start(bf16[1,108,5120]{2,1,0:T(8,128)(2,1)} %param.11) | copy-start | bytes 3317764
  10.8 931.2 %all-reduce.3.cloned.1.call-start = ((), (), s32[]{:S(2)}) async-start(), calls=%async_computation.2 | async-start | bytes 6881280 | tf_op jit(solution)/shard_map/psum | solution.py:85
  354.5 7.9 copy-start
  362.4 371.3 %copy-start.8 = (bf16[1,108,5120]{2,1,0:T(8,128)(2,1)S(1)}, bf16[1,108,5120]{2,1,0:T(8,128)(2,1)}, u32[]{:S(2)}) copy-start(bf16[1,108,5120]{2,1,0:T(8,128)(2,1)} %param.12) | copy-start | bytes 3317764
  733.7 7.6 copy-start.6
  733.7 7.7 copy-start.9
  733.7 15.2 %slice-start = ((s8[10485760]{0:T(1024)(128)(4,1)}), s8[4194304]{0:T(1024)(128)(4,1)S(1)}, s32[]{:S(2)}) async-start(s8[10485760]{0:T(1024)(128)(4,1)} %bitcast.56), calls=%async_computation.3 | async-start | bytes 8388608
  733.8 15.2 %slice-start.1 = ((s8[10485760]{0:T(1024)(128)(4,1)}), s8[4194304]{0:T(1024)(128)(4,1)S(1)}, s32[]{:S(2)}) async-start(s8[10485760]{0:T(1024)(128)(4,1)} %bitcast.56), calls=%async_computation.4 | async-start | bytes 8388608
  741.4 7.5 slice-start.2
  741.4 7.5 copy-start.2
  741.4 7.5 copy-start.10
  749.0 4.4 copy-start.4
  749.0 4.4 copy-start.12
  757.8 184.1 %copy-start.3 = (bf16[1,108,5120]{2,1,0:T(8,128)(2,1)S(1)}, bf16[1,108,5120]{2,1,0:T(8,128)(2,1)}, u32[]{:S(2)}) copy-start(bf16[1,108,5120]{2,1,0:T(8,128)(2,1)} %param.13) | copy-start | bytes 3317764
  941.9 4.1 copy-start.1
  941.9 4.1 copy-start.5
  942.0 4.1 copy-start.7
  942.0 4.1 copy-start.13
  942.0 4.8 copy-start.14
Sparse Core Ops, SparseCore 0:
  10.3 344.1 all-gather.3
  356.3 377.4 all-gather.5
  758.0 183.9 all-reduce.2
where the time goes:
time: 956 us
  waiting for transfers between devices  896 us (94%)
  matrix products  35.3 us (4%)
  between operations  13.9 us (1%)
  other arithmetic  9.76 us (1%)
    all_gather x1, waiting for transfers between devices, per_device(): whole_cot = lax.all_gather(own_cot, 'tensor', axis=0, tiled=True)  368 us
    all_gather x1, waiting for transfers between devices, per_device(): normed = lax.all_gather(normalize(own_rows), 'tensor', axis=0, tiled=True)  344 us
    psum x1, waiting for transfers between devices, per_device(): lax.psum(term_gate, 'island').astype(jnp.float32)  184 us
  transfers between devices with their start and end apart: 3, of which 3 were waited for; matrix products, arithmetic and copies ran while one was open for 1% of the time, Pallas kernels for 0%

commit v1 on v0

--- a/solution.py
+++ b/solution.py
@@ -2,6 +2,7 @@
 import jax.numpy as jnp
 from jax import lax
 from jax.sharding import PartitionSpec as P
+from jax.lax import all_to_all, axis_size
 
 D = 5120
 FF = 6912
@@ -73,7 +74,9 @@
     own_rows = activations[0]
     own_cot = cotangent[0]
     normed = lax.all_gather(normalize(own_rows), "tensor", axis=0, tiled=True)
-    whole_cot = lax.all_gather(own_cot, "tensor", axis=0, tiled=True)
+    back = jnp.stack([own_cot for _ in range(axis_size("tensor"))], 0)
+    later = all_to_all(back, axis_name="tensor", split_axis=0, concat_axis=0)
+    whole_cot = jnp.concatenate(later, 0)
     grad_gate, grad_up, grad_down = block_grads(
         normed, whole_cot, gate_weight[0], up_weight[0], down_weight[0]
     )

time: 956 us -> 698 us (0.73)
  waiting for transfers between devices: 896 us -> 620 us
  starting transfers between devices: 0.12 us -> 13 us
    all_to_all x0 -> x1, waiting for transfers between devices: none -> 409 us  [per_device(): later = all_to_all(back, axis_name='tensor', split_axis=0, concat_axis=0)]
    all_gather x1 -> x0, waiting for transfers between devices: 368 us -> none  [per_device(): whole_cot = lax.all_gather(own_cot, 'tensor', axis=0, tiled=True)]
    all_gather x1, waiting for transfers between devices: 344 us -> 45 us  [per_device(): normed = lax.all_gather(normalize(own_rows), 'tensor', axis=0, tiled=True)]
    psum x1, waiting for transfers between devices: 184 us -> 166 us  [per_device(): lax.psum(term_gate, 'island').astype(jnp.float32)]
    all_to_all x0 -> x1, starting transfers between devices: none -> 12.9 us  [per_device(): later = all_to_all(back, axis_name='tensor', split_axis=0, concat_axis=0)]
where the time goes in v1:
time: 698 us
  waiting for transfers between devices  620 us (89%)
  matrix products  35.9 us (5%)
  between operations  14.2 us (2%)
  starting transfers between devices  13 us (2%)
  other arithmetic  7.93 us (1%)
    all_to_all x1, waiting for transfers between devices, per_device(): later = all_to_all(back, axis_name='tensor', split_axis=0, concat_axis=0)  409 us
    psum x1, waiting for transfers between devices, per_device(): lax.psum(term_gate, 'island').astype(jnp.float32)  166 us
    all_gather x1, waiting for transfers between devices, per_device(): normed = lax.all_gather(normalize(own_rows), 'tensor', axis=0, tiled=True)  45 us
    dot_general x3, matrix products, contract_last(): lax.dot_general(left, right, (((1,), (1,)), ((), ())), preferred_element_...  19.6 us
    dot_general x3, matrix products, contract_first(): lax.dot_general(left, right, (((0,), (0,)), ((), ())), preferred_element_...  16.3 us
  transfers between devices with their start and end apart: 3, of which 3 were waited for; matrix products, arithmetic and copies ran while one was open for 1% of the time, Pallas kernels for 0%

profile of v1, /device:TPU:1, one launch (start us, length us, event | category | flops | bytes accessed | tf_op | source)
XLA Modules:
  0.0 698.0 jit_solution(17461719866586189629)
XLA Ops:
  7.2 6.1 stack.3
  13.3 12.9 %all-to-all-start = ((bf16[64,16,5120]{2,1,0:T(8,128)(2,1)}), bf16[64,16,5120]{2,1,0:T(8,128)(2,1)}, u32[]{:S(2)}, u32[]{:S(2)}) async-start(bf16[64,16,5120]{2,1,0:T(8,128)(2,1)} %stack.3), calls=%async_computation | async-start | bytes 20971520 | tf_op jit(solution)/shard_map/all_to_all | solution.py:78
  26.2 0.0 all-gather.2.cloned.1.call-start
  26.2 0.2 fusion.22
  26.4 0.8 fusion.23
  27.2 0.0 all-gather.2.cloned.1.call-update
  27.2 0.0 all-reduce.3.cloned.1.call-start
  27.2 409.1 %all-to-all-done = bf16[64,16,5120]{2,1,0:T(8,128)(2,1)} async-done(((bf16[64,16,5120]{2,1,0:T(8,128)(2,1)}), bf16[64,16,5120]{2,1,0:T(8,128)(2,1)}, u32[]{:S(2)}, u32[]{:S(2)}) %all-to-all-start) | async-done | bytes 10485792 | tf_op jit(solution)/shard_map/all_to_all | solution.py:78
  436.3 8.4 %convolution_multiply_fusion.5 = f32[1024,108]{0,1:T(8,128)} fusion(bf16[1024,5120]{1,0:T(8,128)(2,1)} %bitcast.2, bf16[1,108,5120]{2,1,0:T(8,128)(2,1)S(1)} %copy-done.8), kind=kOutput, calls=%fused_computation.29 | convolution fusion | flops 1132572672 | bytes 12034048 | tf_op jit(solution)/shard_map/dot_general | solution.py:21
  444.7 45.0 %all-gather.2.cloned.1.call-done = bf16[1024,5120]{1,0:T(8,128)(2,1)} async-done(((bf16[16,5120]{1,0:T(8,128)(2,1)}), bf16[1024,5120]{1,0:T(8,128)(2,1)}) %all-gather.2.cloned.1.call-update) | async-done | bytes 10485776 | tf_op jit(solution)/shard_map/all_gather | solution.py:76
  489.7 7.6 %convolution_multiply_fusion.3 = f32[1024,108]{0,1:T(8,128)S(1)} fusion(bf16[1024,5120]{1,0:T(8,128)(2,1)} %all-gather.2.cloned.1.call-done, bf16[1,108,5120]{2,1,0:T(8,128)(2,1)S(1)} %copy-done.10), kind=kOutput, calls=%fused_computation.27 | convolution fusion | flops 1132572672 | bytes 12034048 | tf_op jit(solution)/shard_map/dot_general | solution.py:21
  497.4 0.0 copy-start.5
  497.4 0.0 copy-start.9
  497.4 3.6 convolution_multiply_fusion.4
  501.0 0.0 copy-start.2
  501.1 7.5 %fusion.13 = (bf16[108,5120]{1,0:T(8,128)(2,1)}, f32[108,5120]{1,0:T(8,128)S(1)}) fusion(bf16[1,108,5120]{2,1,0:T(8,128)(2,1)S(1)} %copy-done.5, bf16[1024,5120]{1,0:T(8,128)(2,1)} %bitcast.2, f32[1024,108]{0,1:T(8,128)S(1)} %convolution_multiply_fusion.4, f32[1024,108]{0,1:T(8,128)S(1)} %convolution_multiply_fusion.3, bf16[1,108,5120]{2,1,0:T(8,128)(2,1)S(1)} %copy-done.9), kind=kOutput, calls=%fused_computation.22 | convolution fusion | flops 1137549312 | bytes 16900096 | tf_op jit(solution)/shard_map/dot_general | solution.py:15
  508.6 0.0 copy-start.3
  508.6 4.3 fusion.7
  513.0 4.4 fusion.10
  517.4 0.0 all-reduce.3.cloned.1.call-update
  517.4 165.9 %all-reduce.3.cloned.1.call-done = (bf16[108,5120]{1,0:T(8,128)(2,1)}, bf16[108,5120]{1,0:T(8,128)(2,1)}, bf16[108,5120]{1,0:T(8,128)(2,1)}) async-done(((bf16[108,5120]{1,0:T(8,128)(2,1)}, bf16[108,5120]{1,0:T(8,128)(2,1)}, bf16[108,5120]{1,0:T(8,128)(2,1)}), (bf16[108,5120]{1,0:T(8,128)(2,1)}, bf16[108,5120]{1,0:T(8,128)(2,1)}, bf16[108,5120]{1,0:T(8,128)(2,1)})) %all-reduce.3.cloned.1.call-update) | async-done | bytes 3317776 | tf_op jit(solution)/shard_map/psum | solution.py:88
  683.4 4.0 fusion.17
  687.4 0.8 copy-done.15
  688.2 3.0 fusion.15
  (30 shorter events, 0.1 us)
Async XLA Ops:
  13.3 13.0 %copy-start.16 = (bf16[1,16,5120]{2,1,0:T(8,128)(2,1)S(1)}, bf16[1,16,5120]{2,1,0:T(8,128)(2,1)}, u32[]{:S(2)}) copy-start(bf16[1,16,5120]{2,1,0:T(8,128)(2,1)} %param.8) | copy-start | bytes 491524
  13.3 423.1 %copy-start.8 = (bf16[1,108,5120]{2,1,0:T(8,128)(2,1)S(1)}, bf16[1,108,5120]{2,1,0:T(8,128)(2,1)}, u32[]{:S(2)}) copy-start(bf16[1,108,5120]{2,1,0:T(8,128)(2,1)} %param.12) | copy-start | bytes 3317764
  13.3 423.1 %all-to-all-start = ((bf16[64,16,5120]{2,1,0:T(8,128)(2,1)}), bf16[64,16,5120]{2,1,0:T(8,128)(2,1)}, u32[]{:S(2)}, u32[]{:S(2)}) async-start(bf16[64,16,5120]{2,1,0:T(8,128)(2,1)} %stack.3), calls=%async_computation | async-start | bytes 20971520 | tf_op jit(solution)/shard_map/all_to_all | solution.py:78
  26.2 463.6 %all-gather.2.cloned.1.call-start = ((), (), s32[]{:S(2)}) async-start(), calls=%async_computation.1 | async-start | bytes 10649600 | tf_op jit(solution)/shard_map/all_gather | solution.py:76
  27.2 656.2 %all-reduce.3.cloned.1.call-start = ((), (), s32[]{:S(2)}) async-start(), calls=%async_computation.2 | async-start | bytes 6881280 | tf_op jit(solution)/shard_map/psum | solution.py:88
  436.3 53.4 %copy-start.10 = (bf16[1,108,5120]{2,1,0:T(8,128)(2,1)S(1)}, bf16[1,108,5120]{2,1,0:T(8,128)(2,1)}, u32[]{:S(2)}) copy-start(bf16[1,108,5120]{2,1,0:T(8,128)(2,1)} %param.10) | copy-start | bytes 3317764
  444.7 52.7 %copy-start.12 = (bf16[1,108,5120]{2,1,0:T(8,128)(2,1)S(1)}, bf16[1,108,5120]{2,1,0:T(8,128)(2,1)}, u32[]{:S(2)}) copy-start(bf16[1,108,5120]{2,1,0:T(8,128)(2,1)} %param.11) | copy-start | bytes 3317764
  489.7 7.6 %copy-start = (bf16[1024,5120]{1,0:T(8,128)(2,1)S(1)}, bf16[1024,5120]{1,0:T(8,128)(2,1)}, u32[]{:S(2)}) copy-start(bf16[1024,5120]{1,0:T(8,128)(2,1)} %all-gather.2.cloned.1.call-done) | copy-start | bytes 31457284
  497.4 3.6 copy-start.5
  497.4 3.6 copy-start.9
  501.0 7.5 %copy-start.2 = (bf16[1,108,5120]{2,1,0:T(8,128)(2,1)S(1)}, bf16[1,108,5120]{2,1,0:T(8,128)(2,1)}, u32[]{:S(2)}) copy-start(bf16[1,108,5120]{2,1,0:T(8,128)(2,1)} %param.13) | copy-start | bytes 3317764
  501.0 7.5 %copy-start.7 = (f32[1024,108]{0,1:T(8,128)S(1)}, f32[1024,108]{0,1:T(8,128)}, u32[]{:S(2)}) copy-start(f32[1024,108]{0,1:T(8,128)} %convolution_multiply_fusion.5) | copy-start | bytes 1327108
  501.1 7.5 %copy-start.11 = (bf16[1,108,5120]{2,1,0:T(8,128)(2,1)S(1)}, bf16[1,108,5120]{2,1,0:T(8,128)(2,1)}, u32[]{:S(2)}) copy-start(bf16[1,108,5120]{2,1,0:T(8,128)(2,1)} %param.10) | copy-start | bytes 3317764
  508.6 4.4 copy-start.3
  508.6 4.4 copy-start.13
  683.4 4.1 copy-start.1
  683.4 4.1 copy-start.4
  683.4 4.1 copy-start.6
  683.4 4.1 copy-start.14
  683.4 4.8 copy-start.15
Sparse Core Ops, SparseCore 0:
  29.3 460.3 all-gather.1
  517.6 165.7 all-reduce.2
